TPU v7x, 256 devices: a whole 4x4x8 slice. The times are simulated.
256 devices in a mesh: hid: 32 (over y, z), wid: 4 (over x), ad: 2 (over core).
Axes of the slice: x: 4, y: 4, z: 8, core: 2. Of those that a mesh axis runs over, the one named last changes fastest.
Arguments:
- activations: bfloat16 [1536, 2, 8192], P(None, None, ('wid', 'ad')), may hold values from -6 to 6
- row_adapter_index: int32 [1536, 2], replicated, may hold values from 0 to 127, as said below
- gate_up_weight: bfloat16 [8192, 2, 14848], P(('wid', 'ad'), None, 'hid'), may hold values from -0.0625 to 0.0625
- down_weight: bfloat16 [14848, 8192], P('hid', ('wid', 'ad')), may hold values from -0.046875 to 0.046875
- adapter_shrink_weight: bfloat16 [128, 2, 64, 8192], P(('hid', 'wid'), 'ad'), may hold values from -0.0625 to 0.0625
- adapter_expand_weight: bfloat16 [128, 2, 64, 14848], P(('hid', 'wid'), 'ad'), may hold values from -0.75 to 0.75
Outputs:
- layer_out: bfloat16 [1536, 2, 8192], P('hid', None, ('wid', 'ad'))
Inputs may be any that keep to these rules, and one draw needn't show every extreme that they name: `row_adapter_index`: call rows 48 * h to 48 * h + 47 of both batches together block h. In every block no adapter is named more than 2 times, and one and the same adapter is named exactly 2 times in every block.
All inputs are finite; a program needn't handle non-finite values.
Results may differ from a plain program's by a relative error of at most 0.0064.
Values may be sent and summed in bfloat16 or wider, within the bound.
No kernel may reach another device: no remote copies, remote signals or barrier semaphores. Data moves between devices by JAX's collectives and lax.ppermute only.
A program may use at most 128 MiB of HBM per device.

v0:
```python
import jax
import jax.numpy as jnp
from jax import lax
from jax.sharding import Mesh, PartitionSpec as P

CHUNKS = 3
Y, Z = (4, 8)
F32 = jnp.float32
BF16 = jnp.bfloat16


def local(activations, row_adapter_index, gate_up_weight, down_weight, shrink, expand):
    hid = lax.axis_index(("y", "z"))
    wid = lax.axis_index("wid")
    ad = lax.axis_index("ad")
    n_hid = Y * Z
    total_rows, batches, width = activations.shape
    rows = total_rows * batches
    block = rows // n_hid
    part = block // CHUNKS
    units = down_weight.shape[0]
    rank = shrink.shape[2]
    slots = 2 * n_hid
    by_owner = expand[0, 0].reshape(rank, n_hid, units).transpose(1, 0, 2)
    expand_all = lax.all_to_all(by_owner, ("y", "z"), split_axis=0, concat_axis=0, tiled=True)

    def to_chunks(flat):
        return flat.reshape((n_hid, CHUNKS, part) + flat.shape[1:]).swapaxes(0, 1)

    acts = activations.reshape(n_hid, CHUNKS, part // 2, 2, width)
    acts = acts.swapaxes(0, 1).reshape(rows, width)
    ids = row_adapter_index.reshape(n_hid, block)
    same = ids[:, :, None] == ids[:, None, :]
    earlier = jnp.arange(block)[None, :] < jnp.arange(block)[:, None]
    place = jnp.sum((same & earlier[None]).astype(jnp.int32), axis=2)
    slot = 2 * jnp.arange(n_hid, dtype=jnp.int32)[:, None] + place
    owner, cls = (ids // 4, ids % 4)
    send_code = jnp.where(owner == hid, cls * slots + slot, -1)
    recv_code = jnp.where(cls == wid, owner * slots + slot, -1)
    send_code = to_chunks(send_code.reshape(rows)).reshape(rows)
    recv_code = to_chunks(recv_code.reshape(rows)).reshape(CHUNKS, rows // CHUNKS)
    pick = (jnp.arange(4 * slots, dtype=jnp.int32)[:, None] == send_code[None, :]).astype(BF16)
    picked = jnp.dot(pick, acts, preferred_element_type=F32).astype(BF16)
    picked = picked.reshape(4, 1, slots, width)
    picked = jnp.broadcast_to(picked, (4, 2, slots, width)).reshape(8, slots, width)
    got = lax.all_to_all(picked, ("wid", "ad"), split_axis=0, concat_axis=0, tiled=True)
    inner = jnp.einsum(
        "xsf,jxf->sj", got, shrink[0, 0].reshape(rank, 8, width), preferred_element_type=F32
    ).astype(BF16)
    inner_all = lax.all_to_all(
        jnp.broadcast_to(inner[None], (n_hid, slots, rank)),
        ("y", "z"),
        split_axis=0,
        concat_axis=0,
        tiled=True,
    )
    terms = (
        jnp.einsum("hsj,hju->hsu", inner_all, expand_all, preferred_element_type=F32)
        .astype(BF16)
        .reshape(n_hid * slots, units)
    )
    weights = gate_up_weight.transpose(1, 0, 2)
    chunk_rows = rows // CHUNKS
    half = chunk_rows // 2
    quarter = half // 4
    is_mine = (jnp.arange(2) == ad)[:, None, None]
    swap = [(0, 1), (1, 0)]
    acts = acts.reshape(CHUNKS, chunk_rows, width)
    outs = []
    for c in range(CHUNKS):
        base = jnp.einsum("rd,pdu->pru", acts[c], weights, preferred_element_type=F32)
        place_rows = (
            recv_code[c][:, None] == jnp.arange(n_hid * slots, dtype=jnp.int32)[None, :]
        ).astype(BF16)
        delta = jnp.dot(place_rows, terms, preferred_element_type=F32).astype(BF16)
        value = base + jnp.where(is_mine, delta.astype(F32)[None], 0.0)
        away = lax.dynamic_slice_in_dim(value, (1 - ad) * half, half, 1).astype(BF16)
        keep = lax.dynamic_slice_in_dim(value, ad * half, half, 1)
        pair = keep + lax.ppermute(away, "ad", swap).astype(F32)
        pair = pair.astype(BF16).reshape(2, 4, quarter, units).swapaxes(0, 1)
        parts = lax.all_to_all(pair, "wid", split_axis=0, concat_axis=0, tiled=True)
        summed = jnp.sum(parts.astype(F32), axis=0)
        hidden = (jax.nn.silu(summed[0]) * summed[1]).astype(BF16)
        hidden = lax.all_gather(hidden, ("ad", "wid"), axis=0, tiled=True)
        partial = jnp.dot(hidden, down_weight, preferred_element_type=F32).astype(BF16)
        partial = lax.psum_scatter(partial, "y", scatter_dimension=0, tiled=True)
        outs.append(lax.psum_scatter(partial, "z", scatter_dimension=0, tiled=True))
    out = jnp.concatenate(outs, axis=0)
    return out.reshape(total_rows // n_hid, batches, -1)


def solution(mesh):
    grid = Mesh(mesh.devices.reshape(Y, Z, 4, 2), ("y", "z", "wid", "ad"))
    hid = ("y", "z")
    in_specs = (
        P(None, None, ("wid", "ad")),
        P(),
        P(("wid", "ad"), None, hid),
        P(hid, ("wid", "ad")),
        P(("y", "z", "wid"), "ad", None, None),
        P(("y", "z", "wid"), "ad", None, None),
    )
    return jax.shard_map(
        local, mesh=grid, in_specs=in_specs, out_specs=P(hid, None, ("wid", "ad")), check_vma=False
    )
```

profile of v0, /device:TPU:2, one launch (start us, length us, event | category | flops | bytes accessed | tf_op | source)
XLA Modules:
  0.0 464.6 jit_solution(17052631867190961436)
XLA Ops:
  10.0 6.8 %copy.57 = bf16[32,3,16,2,1024]{4,3,2,0,1:T(2,128)(2,1)} copy(bf16[32,3,16,2,1024]{4,3,2,1,0:T(2,128)(2,1)} %bitcast.107) | data formatting | bytes 12582912 | tf_op jit(solution)/shard_map/reshape | solution.py:30
  16.7 10.2 %reshape.89 = bf16[3072,1024]{1,0:T(8,128)(2,1)} reshape(bf16[3,32,16,2,1024]{4,3,2,1,0:T(2,128)(2,1)} %bitcast.104) | data formatting | bytes 12582912 | tf_op jit(solution)/shard_map/reshape | solution.py:31
  26.9 4.6 fusion.17
  32.7 6.4 %all-to-all-start = ((bf16[8,64,1024]{2,1,0:T(8,128)(2,1)}), bf16[8,64,1024]{2,1,0:T(8,128)(2,1)}, u32[]{:S(2)}, u32[]{:S(2)}) async-start(bf16[8,64,1024]{2,1,0:T(8,128)(2,1)} %bitcast.7), calls=%async_computation | async-start | bytes 2097152 | tf_op jit(solution)/shard_map/all_to_all | solution.py:46
  40.7 13.0 %all-to-all-done = bf16[8,64,1024]{2,1,0:T(8,128)(2,1)} async-done(((bf16[8,64,1024]{2,1,0:T(8,128)(2,1)}), bf16[8,64,1024]{2,1,0:T(8,128)(2,1)}, u32[]{:S(2)}, u32[]{:S(2)}) %all-to-all-start) | async-done | bytes 1048608 | tf_op jit(solution)/shard_map/all_to_all | solution.py:46
  53.6 2.9 fusion.18
  57.8 9.9 %all-to-all-start.1 = ((bf16[32,2,2048]{2,1,0:T(2,128)(2,1)}), bf16[32,2,2048]{2,1,0:T(2,128)(2,1)S(1)}, u32[]{:S(2)}, u32[]{:S(2)}) async-start(bf16[32,2,2048]{2,1,0:T(2,128)(2,1)} %reshape.120), calls=%async_computation.1 | async-start | bytes 524288 | tf_op jit(solution)/shard_map/all_to_all | solution.py:50
  67.7 6.7 %reshape_squeeze.7 = bf16[64,32,464]{2,1,0:T(8,128)(2,1)} reshape(bf16[1,1,64,14848]{3,2,1,0:T(8,128)(2,1)} %param.11) | data formatting | bytes 3801088 | tf_op jit(solution)/shard_map/reshape;squeeze | solution.py:24
  74.4 4.1 copy.58
  79.8 8.8 %all-to-all-start.2 = ((bf16[32,64,464]{2,1,0:T(8,128)(2,1)}), bf16[32,64,464]{2,1,0:T(8,128)(2,1)}, u32[]{:S(2)}, u32[]{:S(2)}) async-start(bf16[32,64,464]{2,1,0:T(8,128)(2,1)} %bitcast.106), calls=%async_computation.2 | async-start | bytes 4194304 | tf_op jit(solution)/shard_map/all_to_all | solution.py:25
  88.8 7.7 %fusion.30 = (bf16[1,32,16,2,1024]{4,3,2,1,0:T(2,128)(2,1)}, bf16[1,32,16,2,1024]{4,3,2,1,0:T(2,128)(2,1)}, bf16[1,32,16,2,1024]{4,3,2,1,0:T(2,128)(2,1)}) fusion(bf16[3,32,16,2,1024]{4,3,2,1,0:T(2,128)(2,1)} %bitcast.105), kind=kLoop, calls=%fused_computation.79 | loop fusion | bytes 12582912 | tf_op jit(solution)/shard_map/slice | solution.py:71
  96.5 4.1 reshape.96
  100.9 36.9 %all-to-all-done.2 = bf16[32,64,464]{2,1,0:T(8,128)(2,1)} async-done(((bf16[32,64,464]{2,1,0:T(8,128)(2,1)}), bf16[32,64,464]{2,1,0:T(8,128)(2,1)}, u32[]{:S(2)}, u32[]{:S(2)}) %all-to-all-start.2) | async-done | bytes 1900576 | tf_op jit(solution)/shard_map/all_to_all | solution.py:25
  148.2 2.6 collective-permute-done
  150.8 3.0 bitcast_bitcast_fusion.2
  153.8 4.9 %all-to-all-start.3 = ((bf16[4,2,128,464]{2,3,1,0:T(8,128)(2,1)}), bf16[4,2,128,464]{2,3,1,0:T(8,128)(2,1)S(1)}, u32[]{:S(2)}, u32[]{:S(2)}) async-start(bf16[4,2,128,464]{2,3,1,0:T(8,128)(2,1)} %bitcast_bitcast_fusion.2), calls=%async_computation.3 | async-start | bytes 1900544 | tf_op jit(solution)/shard_map/all_to_all | solution.py:81
  158.8 4.1 reshape.99
  162.9 9.0 %all-to-all-done.3 = bf16[4,2,128,464]{2,3,1,0:T(8,128)(2,1)S(1)} async-done(((bf16[4,2,128,464]{2,3,1,0:T(8,128)(2,1)}), bf16[4,2,128,464]{2,3,1,0:T(8,128)(2,1)S(1)}, u32[]{:S(2)}, u32[]{:S(2)}) %all-to-all-start.3) | async-done | bytes 950304 | tf_op jit(solution)/shard_map/all_to_all | solution.py:81
  172.1 24.2 %all_gather.9 = bf16[1024,464]{0,1:T(8,128)(2,1)S(1)} all-gather(bf16[128,464]{0,1:T(8,128)(2,1)S(1)} %fusion.28), channel_id=1, replica_groups=mesh['y'=4,'z'=8,'wid'=4,'ad'=2] {'ad','wid'}, dimensions={0}, use_global_device_ids=true | all-gather | bytes 1069056 | tf_op jit(solution)/shard_map/all_gather | solution.py:84
  196.4 2.6 convolution_convert_fusion.2
  199.0 4.1 fusion.12
  209.7 4.9 %all-to-all-start.5 = ((bf16[4,2,128,464]{2,3,1,0:T(8,128)(2,1)}), bf16[4,2,128,464]{2,3,1,0:T(8,128)(2,1)S(1)}, u32[]{:S(2)}, u32[]{:S(2)}) async-start(bf16[4,2,128,464]{2,3,1,0:T(8,128)(2,1)} %bitcast_bitcast_fusion), calls=%async_computation.9 | async-start | bytes 1900544 | tf_op jit(solution)/shard_map/all_to_all | solution.py:81
  214.7 4.1 reshape.98
  218.8 9.2 %all-to-all-done.5 = bf16[4,2,128,464]{2,3,1,0:T(8,128)(2,1)S(1)} async-done(((bf16[4,2,128,464]{2,3,1,0:T(8,128)(2,1)}), bf16[4,2,128,464]{2,3,1,0:T(8,128)(2,1)S(1)}, u32[]{:S(2)}, u32[]{:S(2)}) %all-to-all-start.5) | async-done | bytes 950304 | tf_op jit(solution)/shard_map/all_to_all | solution.py:81
  228.2 24.1 %all_gather.11 = bf16[1024,464]{0,1:T(8,128)(2,1)S(1)} all-gather(bf16[128,464]{0,1:T(8,128)(2,1)S(1)} %fusion.24), channel_id=1, replica_groups=mesh['y'=4,'z'=8,'wid'=4,'ad'=2] {'ad','wid'}, dimensions={0}, use_global_device_ids=true | all-gather | bytes 1069056 | tf_op jit(solution)/shard_map/all_gather | solution.py:84
  255.3 4.1 fusion.14
  265.3 17.4 %all_to_all.30 = bf16[4,2,128,464]{2,3,1,0:T(8,128)(2,1)S(1)} all-to-all(bf16[4,2,128,464]{2,3,1,0:T(8,128)(2,1)S(1)} %bitcast_bitcast_fusion.1), channel_id=1, replica_groups=mesh['y'=4,'z'=8,'wid'=4,'ad'=2] {'wid'}, dimensions={0} | all-to-all | bytes 1900544 | tf_op jit(solution)/shard_map/all_to_all | solution.py:81
  282.9 23.9 %all_gather.10 = bf16[1024,464]{0,1:T(8,128)(2,1)S(1)} all-gather(bf16[128,464]{0,1:T(8,128)(2,1)S(1)} %fusion.26), channel_id=1, replica_groups=mesh['y'=4,'z'=8,'wid'=4,'ad'=2] {'ad','wid'}, dimensions={0}, use_global_device_ids=true | all-gather | bytes 1069056 | tf_op jit(solution)/shard_map/all_gather | solution.py:84
  310.6 28.0 %reduce-scatter.11.cloned.1.call-done = bf16[256,1024]{1,0:T(8,128)(2,1)} async-done(((bf16[1024,1024]{1,0:T(8,128)(2,1)}), bf16[256,1024]{1,0:T(8,128)(2,1)}) %reduce-scatter.11.cloned.1.call-update) | async-done | bytes 524304 | tf_op jit(solution)/shard_map/reduce_scatter | solution.py:86
  338.7 39.8 %reduce-scatter.9.cloned.1.call-done = bf16[32,1024]{1,0:T(8,128)(2,1)} async-done(((bf16[256,1024]{1,0:T(8,128)(2,1)}), bf16[32,1024]{1,0:T(8,128)(2,1)}) %reduce-scatter.9.cloned.1.call-update) | async-done | bytes 65552 | tf_op jit(solution)/shard_map/reduce_scatter | solution.py:87
  378.5 38.8 %reduce-scatter.17.cloned.1.call-done = bf16[32,1024]{1,0:T(8,128)(2,1)} async-done(((bf16[256,1024]{1,0:T(8,128)(2,1)}), bf16[32,1024]{1,0:T(8,128)(2,1)}) %reduce-scatter.17.cloned.1.call-update) | async-done | bytes 65552 | tf_op jit(solution)/shard_map/reduce_scatter | solution.py:87
  417.3 38.8 %reduce-scatter.13.cloned.1.call-done = bf16[32,1024]{1,0:T(8,128)(2,1)} async-done(((bf16[256,1024]{1,0:T(8,128)(2,1)}), bf16[32,1024]{1,0:T(8,128)(2,1)}) %reduce-scatter.13.cloned.1.call-update) | async-done | bytes 65552 | tf_op jit(solution)/shard_map/reduce_scatter | solution.py:87
  (80 shorter events, 41.0 us)
Async XLA Ops:
  6.5 137.3 %copy-start = (bf16[1024,2,464]{0,2,1:T(8,128)(2,1)S(1)}, bf16[1024,2,464]{0,2,1:T(8,128)(2,1)}, u32[]{:S(2)}) copy-start(bf16[1024,2,464]{0,2,1:T(8,128)(2,1)} %param.8) | copy-start | bytes 5701636
  31.5 7.5 %copy-start.6 = (bf16[1,1,64,8192]{3,2,1,0:T(8,128)(2,1)S(1)}, bf16[1,1,64,8192]{3,2,1,0:T(8,128)(2,1)}, u32[]{:S(2)}) copy-start(bf16[1,1,64,8192]{3,2,1,0:T(8,128)(2,1)} %param.10) | copy-start | bytes 3145732
  32.7 21.0 %all-to-all-start = ((bf16[8,64,1024]{2,1,0:T(8,128)(2,1)}), bf16[8,64,1024]{2,1,0:T(8,128)(2,1)}, u32[]{:S(2)}, u32[]{:S(2)}) async-start(bf16[8,64,1024]{2,1,0:T(8,128)(2,1)} %bitcast.7), calls=%async_computation | async-start | bytes 2097152 | tf_op jit(solution)/shard_map/all_to_all | solution.py:46
  57.8 22.0 %all-to-all-start.1 = ((bf16[32,2,2048]{2,1,0:T(2,128)(2,1)}), bf16[32,2,2048]{2,1,0:T(2,128)(2,1)S(1)}, u32[]{:S(2)}, u32[]{:S(2)}) async-start(bf16[32,2,2048]{2,1,0:T(2,128)(2,1)} %reshape.120), calls=%async_computation.1 | async-start | bytes 524288 | tf_op jit(solution)/shard_map/all_to_all | solution.py:50
  79.8 58.0 %all-to-all-start.2 = ((bf16[32,64,464]{2,1,0:T(8,128)(2,1)}), bf16[32,64,464]{2,1,0:T(8,128)(2,1)}, u32[]{:S(2)}, u32[]{:S(2)}) async-start(bf16[32,64,464]{2,1,0:T(8,128)(2,1)} %bitcast.106), calls=%async_computation.2 | async-start | bytes 4194304 | tf_op jit(solution)/shard_map/all_to_all | solution.py:25
  140.1 1.3 copy-start.2
  141.4 2.4 copy-start.5
  146.1 1.8 copy-start.1
  148.0 2.7 collective-permute-start
  153.8 18.1 %all-to-all-start.3 = ((bf16[4,2,128,464]{2,3,1,0:T(8,128)(2,1)}), bf16[4,2,128,464]{2,3,1,0:T(8,128)(2,1)S(1)}, u32[]{:S(2)}, u32[]{:S(2)}) async-start(bf16[4,2,128,464]{2,3,1,0:T(8,128)(2,1)} %bitcast_bitcast_fusion.2), calls=%async_computation.3 | async-start | bytes 1900544 | tf_op jit(solution)/shard_map/all_to_all | solution.py:81
  158.7 150.8 %reduce-scatter.7.cloned.1.call-start = ((), (), s32[]{:S(2)}) async-start(), calls=%async_computation.12 | async-start | bytes 2621440 | tf_op jit(solution)/shard_map/reduce_scatter | solution.py:86
  171.9 24.5 %copy-start.7 = (bf16[464,1024]{1,0:T(8,128)(2,1)S(1)}, bf16[464,1024]{1,0:T(8,128)(2,1)}, u32[]{:S(2)}) copy-start(bf16[464,1024]{1,0:T(8,128)(2,1)} %param.9) | copy-start | bytes 2850820
  199.0 4.2 copy-start.4
  205.5 3.0 collective-permute-start.2
  209.7 18.3 %all-to-all-start.5 = ((bf16[4,2,128,464]{2,3,1,0:T(8,128)(2,1)}), bf16[4,2,128,464]{2,3,1,0:T(8,128)(2,1)S(1)}, u32[]{:S(2)}, u32[]{:S(2)}) async-start(bf16[4,2,128,464]{2,3,1,0:T(8,128)(2,1)} %bitcast_bitcast_fusion), calls=%async_computation.9 | async-start | bytes 1900544 | tf_op jit(solution)/shard_map/all_to_all | solution.py:81
  214.6 95.5 %reduce-scatter.15.cloned.1.call-start = ((), (), s32[]{:S(2)}) async-start(), calls=%async_computation.16 | async-start | bytes 2621440 | tf_op jit(solution)/shard_map/reduce_scatter | solution.py:86
  228.0 24.3 %copy-start.8 = (bf16[464,1024]{1,0:T(8,128)(2,1)S(1)}, bf16[464,1024]{1,0:T(8,128)(2,1)}, u32[]{:S(2)}) copy-start(bf16[464,1024]{1,0:T(8,128)(2,1)} %param.9) | copy-start | bytes 2850820
  254.9 83.7 %reduce-scatter.11.cloned.1.call-start = ((), (), s32[]{:S(2)}) async-start(), calls=%async_computation.14 | async-start | bytes 2621440 | tf_op jit(solution)/shard_map/reduce_scatter | solution.py:86
  255.2 4.2 copy-start.3
  261.7 3.3 collective-permute-start.1
  265.3 41.5 %copy-start.9 = (bf16[464,1024]{1,0:T(8,128)(2,1)S(1)}, bf16[464,1024]{1,0:T(8,128)(2,1)}, u32[]{:S(2)}) copy-start(bf16[464,1024]{1,0:T(8,128)(2,1)} %param.9) | copy-start | bytes 2850820
  309.4 69.1 %reduce-scatter.9.cloned.1.call-start = ((), (), s32[]{:S(2)}) async-start(), calls=%async_computation.13 | async-start | bytes 589824 | tf_op jit(solution)/shard_map/reduce_scatter | solution.py:87
  310.0 107.3 %reduce-scatter.17.cloned.1.call-start = ((), (), s32[]{:S(2)}) async-start(), calls=%async_computation.17 | async-start | bytes 589824 | tf_op jit(solution)/shard_map/reduce_scatter | solution.py:87
  310.6 145.5 %reduce-scatter.13.cloned.1.call-start = ((), (), s32[]{:S(2)}) async-start(), calls=%async_computation.15 | async-start | bytes 589824 | tf_op jit(solution)/shard_map/reduce_scatter | solution.py:87
Sparse Core Ops, SparseCore 0:
  199.1 29.3 reduce-scatter.6
  255.1 29.7 reduce-scatter.14
  309.5 29.0 reduce-scatter.10
  341.0 37.4 reduce-scatter.8
  380.9 36.3 reduce-scatter.16
  419.7 36.3 reduce-scatter.12
where the time goes:
time: 466 us; the launch traced here: 465 us
  waiting for transfers between devices  223 us (48%)
  blocking collectives  89.6 us (19%)
  local copies, waits for them, and re-layouts  58.9 us (13%)
  starting transfers between devices  37.5 us (8%)
  matrix products  34.8 us (7%)
  between operations  13.8 us (3%)
  other arithmetic  7.22 us (2%)
    reduce_scatter x3, waiting for transfers between devices, local(): outs.append(lax.psum_scatter(partial, 'z', scatter_dimension=0, tiled=True))  117 us
    all_gather x3, blocking collectives, local(): hidden = lax.all_gather(hidden, ('ad', 'wid'), axis=0, tiled=True)  72.3 us
    all_to_all x1, waiting for transfers between devices, local(): lax.all_to_all(by_owner, ('y', 'z'), split_axis=0, concat_axis=0, tiled=T...  36.9 us
    reduce_scatter x3, waiting for transfers between devices, local(): partial = lax.psum_scatter(partial, 'y', scatter_dimension=0, tiled=True)  28.1 us
    all_to_all x2, waiting for transfers between devices, local(): parts = lax.all_to_all(pair, 'wid', split_axis=0, concat_axis=0, tiled=True)  18.2 us
    all_to_all x1, blocking collectives, local(): parts = lax.all_to_all(pair, 'wid', split_axis=0, concat_axis=0, tiled=True)  17.4 us
    all_to_all x1, waiting for transfers between devices, local(): lax.all_to_all(picked, ('wid', 'ad'), split_axis=0, concat_axis=0, tiled=...  13 us
    squeeze x3, local copies, waits for them, and re-layouts, local(): acts[c]  12.4 us
  transfers between devices with their start and end apart: 14, of which 12 were waited for; matrix products, arithmetic and copies ran while one was open for 11% of the time, Pallas kernels for 0%

commit v1 on v0

--- a/solution.py
+++ b/solution.py
@@ -81,7 +81,10 @@
         parts = lax.all_to_all(pair, "wid", split_axis=0, concat_axis=0, tiled=True)
         summed = jnp.sum(parts.astype(F32), axis=0)
         hidden = (jax.nn.silu(summed[0]) * summed[1]).astype(BF16)
-        hidden = lax.all_gather(hidden, ("ad", "wid"), axis=0, tiled=True)
+        hidden = jnp.concatenate(
+            lax.all_to_all(jnp.stack([hidden] * lax.axis_size(("ad", "wid"))), ("ad", "wid"), 0, 0),
+            axis=0,
+        )
         partial = jnp.dot(hidden, down_weight, preferred_element_type=F32).astype(BF16)
         partial = lax.psum_scatter(partial, "y", scatter_dimension=0, tiled=True)
         outs.append(lax.psum_scatter(partial, "z", scatter_dimension=0, tiled=True))

time: 466 us -> 441 us (0.946)
  blocking collectives: 89.6 us -> 68.4 us
  waiting for transfers between devices: 223 us -> 211 us
  matrix products: 34.8 us -> 43.7 us
    all_gather x3 -> x0, blocking collectives: 72.3 us -> none  [local(): hidden = lax.all_gather(hidden, ('ad', 'wid'), axis=0, tiled=True)]
    all_to_all x1 -> x3, blocking collectives: 17.4 us -> 51.2 us  [local(): parts = lax.all_to_all(pair, 'wid', split_axis=0, concat_axis=0, tiled=True)]
    all_to_all x0 -> x1, blocking collectives: none -> 17.2 us  [local(): lax.all_to_all(jnp.stack([hidden] * lax.axis_size(('ad', 'wid'))), ('ad',...]
    all_to_all x2, waiting for transfers between devices: 18.2 us -> 6.79 us  [local(): lax.all_to_all(jnp.stack([hidden] * lax.axis_size(('ad', 'wid'))), ('ad',...]
  transfers between devices with their start and end apart: 14 -> 14, of which waited for: 12 -> 12; matrix products, arithmetic and copies ran while one was open for 11% -> 14% of each run, Pallas kernels for 0% -> 0%
where the time goes in v1:
time: 441 us; the launch traced here: 440 us
  waiting for transfers between devices  211 us (48%)
  blocking collectives  68.4 us (16%)
  local copies, waits for them, and re-layouts  61.1 us (14%)
  matrix products  43.7 us (10%)
  starting transfers between devices  36.3 us (8%)
  between operations  13.8 us (3%)
  other arithmetic  5.29 us (1%)
    reduce_scatter x3, waiting for transfers between devices, local(): outs.append(lax.psum_scatter(partial, 'z', scatter_dimension=0, tiled=True))  117 us
    all_to_all x3, blocking collectives, local(): parts = lax.all_to_all(pair, 'wid', split_axis=0, concat_axis=0, tiled=True)  51.2 us
    all_to_all x1, waiting for transfers between devices, local(): lax.all_to_all(by_owner, ('y', 'z'), split_axis=0, concat_axis=0, tiled=T...  36.9 us
    reduce_scatter x3, waiting for transfers between devices, local(): partial = lax.psum_scatter(partial, 'y', scatter_dimension=0, tiled=True)  27.9 us
    all_to_all x1, blocking collectives, local(): lax.all_to_all(jnp.stack([hidden] * lax.axis_size(('ad', 'wid'))), ('ad',...  17.2 us
    dot_general x3, matrix products, local(): delta = jnp.dot(place_rows, terms, preferred_element_type=F32).astype(BF16)  13 us
    all_to_all x1, waiting for transfers between devices, local(): lax.all_to_all(picked, ('wid', 'ad'), split_axis=0, concat_axis=0, tiled=...  13 us
    squeeze x3, local copies, waits for them, and re-layouts, local(): acts[c]  12.4 us
  transfers between devices with their start and end apart: 14, of which 12 were waited for; matrix products, arithmetic and copies ran while one was open for 14% of the time, Pallas kernels for 0%

profile of v1, /device:TPU:2, one launch (start us, length us, event | category | flops | bytes accessed | tf_op | source)
XLA Modules:
  0.0 439.7 jit_solution(9856583019249585108)
XLA Ops:
  10.0 6.8 %copy.90 = bf16[32,3,16,2,1024]{4,3,2,0,1:T(2,128)(2,1)} copy(bf16[32,3,16,2,1024]{4,3,2,1,0:T(2,128)(2,1)} %bitcast.101) | data formatting | bytes 12582912 | tf_op jit(solution)/shard_map/reshape | solution.py:30
  16.8 10.2 %reshape.101 = bf16[3072,1024]{1,0:T(8,128)(2,1)} reshape(bf16[3,32,16,2,1024]{4,3,2,1,0:T(2,128)(2,1)} %bitcast.98) | data formatting | bytes 12582912 | tf_op jit(solution)/shard_map/reshape | solution.py:31
  27.0 4.6 %fusion.17 = bf16[256,1024]{1,0:T(8,128)(2,1)S(1)} fusion(bf16[3072,1024]{1,0:T(8,128)(2,1)} %reshape.101, s32[3072]{0:T(1024)S(1)} %eq.116), kind=kOutput, calls=%fused_computation.40 | convolution fusion | flops 1611661312 | bytes 6828032 | tf_op jit(solution)/shard_map/dot_general | solution.py:43
  32.7 6.4 %all-to-all-start = ((bf16[8,64,1024]{2,1,0:T(8,128)(2,1)}), bf16[8,64,1024]{2,1,0:T(8,128)(2,1)}, u32[]{:S(2)}, u32[]{:S(2)}) async-start(bf16[8,64,1024]{2,1,0:T(8,128)(2,1)} %bitcast.7), calls=%async_computation | async-start | bytes 2097152 | tf_op jit(solution)/shard_map/all_to_all | solution.py:46
  40.7 13.0 %all-to-all-done = bf16[8,64,1024]{2,1,0:T(8,128)(2,1)} async-done(((bf16[8,64,1024]{2,1,0:T(8,128)(2,1)}), bf16[8,64,1024]{2,1,0:T(8,128)(2,1)}, u32[]{:S(2)}, u32[]{:S(2)}) %all-to-all-start) | async-done | bytes 1048608 | tf_op jit(solution)/shard_map/all_to_all | solution.py:46
  57.8 9.9 %all-to-all-start.1 = ((bf16[32,2,2048]{2,1,0:T(2,128)(2,1)}), bf16[32,2,2048]{2,1,0:T(2,128)(2,1)S(1)}, u32[]{:S(2)}, u32[]{:S(2)}) async-start(bf16[32,2,2048]{2,1,0:T(2,128)(2,1)} %reshape.135), calls=%async_computation.1 | async-start | bytes 524288 | tf_op jit(solution)/shard_map/all_to_all | solution.py:50
  67.7 6.6 %reshape_squeeze.7 = bf16[64,32,464]{2,1,0:T(8,128)(2,1)} reshape(bf16[1,1,64,14848]{3,2,1,0:T(8,128)(2,1)} %param.11) | data formatting | bytes 3801088 | tf_op jit(solution)/shard_map/reshape;squeeze | solution.py:24
  74.4 4.1 copy.91
  79.8 8.7 %all-to-all-start.2 = ((bf16[32,64,464]{2,1,0:T(8,128)(2,1)}), bf16[32,64,464]{2,1,0:T(8,128)(2,1)}, u32[]{:S(2)}, u32[]{:S(2)}) async-start(bf16[32,64,464]{2,1,0:T(8,128)(2,1)} %bitcast.100), calls=%async_computation.2 | async-start | bytes 4194304 | tf_op jit(solution)/shard_map/all_to_all | solution.py:25
  88.7 7.7 %fusion.36 = (bf16[1,32,16,2,1024]{4,3,2,1,0:T(2,128)(2,1)}, bf16[1,32,16,2,1024]{4,3,2,1,0:T(2,128)(2,1)}, bf16[1,32,16,2,1024]{4,3,2,1,0:T(2,128)(2,1)}) fusion(bf16[3,32,16,2,1024]{4,3,2,1,0:T(2,128)(2,1)} %bitcast.99), kind=kLoop, calls=%fused_computation.82 | loop fusion | bytes 12582912 | tf_op jit(solution)/shard_map/slice | solution.py:71
  96.4 4.1 reshape.111
  100.9 36.9 %all-to-all-done.2 = bf16[32,64,464]{2,1,0:T(8,128)(2,1)} async-done(((bf16[32,64,464]{2,1,0:T(8,128)(2,1)}), bf16[32,64,464]{2,1,0:T(8,128)(2,1)}, u32[]{:S(2)}, u32[]{:S(2)}) %all-to-all-start.2) | async-done | bytes 1900576 | tf_op jit(solution)/shard_map/all_to_all | solution.py:25
  152.8 17.0 %all_to_all.45 = bf16[4,2,128,464]{2,3,1,0:T(8,128)(2,1)S(1)} all-to-all(bf16[4,2,128,464]{2,3,1,0:T(8,128)(2,1)S(1)} %bitcast_bitcast_fusion.2), channel_id=1, replica_groups=mesh['y'=4,'z'=8,'wid'=4,'ad'=2] {'wid'}, dimensions={0} | all-to-all | bytes 1900544 | tf_op jit(solution)/shard_map/all_to_all | solution.py:81
  171.0 4.9 %all-to-all-start.4 = ((bf16[8,128,464]{1,2,0:T(8,128)(2,1)}), bf16[8,128,464]{1,2,0:T(8,128)(2,1)S(1)}, u32[]{:S(2)}, u32[]{:S(2)}) async-start(bf16[8,128,464]{1,2,0:T(8,128)(2,1)} %stack.13), calls=%async_computation.4 | async-start | bytes 1900544 | tf_op jit(solution)/shard_map/all_to_all | solution.py:85
  176.0 4.1 reshape.114
  180.2 5.3 %fusion.12 = f32[1024,464]{0,1:T(8,128)} fusion(bf16[2048,464]{1,0:T(8,128)(2,1)} %bitcast.103, s32[1024]{0:T(1024)S(1)} %eq.123), kind=kOutput, calls=%fused_computation.35 | convolution fusion | flops 1949204480 | bytes 3805184 | tf_op jit(solution)/shard_map/dot_general | solution.py:75
  185.5 3.4 all-to-all-done.4
  188.9 3.8 convolution_convert_fusion.2
  192.7 4.3 bitcast_add_fusion
  200.0 17.1 %all_to_all.46 = bf16[4,2,128,464]{2,3,1,0:T(8,128)(2,1)S(1)} all-to-all(bf16[4,2,128,464]{2,3,1,0:T(8,128)(2,1)S(1)} %bitcast_bitcast_fusion), channel_id=1, replica_groups=mesh['y'=4,'z'=8,'wid'=4,'ad'=2] {'wid'}, dimensions={0} | all-to-all | bytes 1900544 | tf_op jit(solution)/shard_map/all_to_all | solution.py:81
  218.4 4.9 %all-to-all-start.8 = ((bf16[8,128,464]{1,2,0:T(8,128)(2,1)}), bf16[8,128,464]{1,2,0:T(8,128)(2,1)S(1)}, u32[]{:S(2)}, u32[]{:S(2)}) async-start(bf16[8,128,464]{1,2,0:T(8,128)(2,1)} %stack.17), calls=%async_computation.12 | async-start | bytes 1900544 | tf_op jit(solution)/shard_map/all_to_all | solution.py:85
  223.4 4.2 reshape.113
  227.5 5.3 %fusion.14 = f32[1024,464]{0,1:T(8,128)} fusion(bf16[2048,464]{1,0:T(8,128)(2,1)} %bitcast.104, s32[1024]{0:T(1024)S(1)} %eq.119), kind=kOutput, calls=%fused_computation.37 | convolution fusion | flops 1949204480 | bytes 3805184 | tf_op jit(solution)/shard_map/dot_general | solution.py:75
  232.8 3.4 all-to-all-done.8
  236.2 3.8 convolution_convert_fusion
  240.3 4.3 bitcast_add_fusion.1
  247.6 17.1 %all_to_all.47 = bf16[4,2,128,464]{2,3,1,0:T(8,128)(2,1)S(1)} all-to-all(bf16[4,2,128,464]{2,3,1,0:T(8,128)(2,1)S(1)} %bitcast_bitcast_fusion.1), channel_id=1, replica_groups=mesh['y'=4,'z'=8,'wid'=4,'ad'=2] {'wid'}, dimensions={0} | all-to-all | bytes 1900544 | tf_op jit(solution)/shard_map/all_to_all | solution.py:81
  265.1 17.2 %all_to_all.48 = bf16[8,128,464]{1,2,0:T(8,128)(2,1)S(1)} all-to-all(bf16[8,128,464]{1,2,0:T(8,128)(2,1)S(1)} %stack.15), channel_id=1, replica_groups=mesh['y'=4,'z'=8,'wid'=4,'ad'=2] {'ad','wid'}, dimensions={0} | all-to-all | bytes 1900544 | tf_op jit(solution)/shard_map/all_to_all | solution.py:85
  286.2 27.8 %reduce-scatter.11.cloned.1.call-done = bf16[256,1024]{1,0:T(8,128)(2,1)} async-done(((bf16[1024,1024]{1,0:T(8,128)(2,1)}), bf16[256,1024]{1,0:T(8,128)(2,1)}) %reduce-scatter.11.cloned.1.call-update) | async-done | bytes 524304 | tf_op jit(solution)/shard_map/reduce_scatter | solution.py:89
  314.0 39.8 %reduce-scatter.9.cloned.1.call-done = bf16[32,1024]{1,0:T(8,128)(2,1)} async-done(((bf16[256,1024]{1,0:T(8,128)(2,1)}), bf16[32,1024]{1,0:T(8,128)(2,1)}) %reduce-scatter.9.cloned.1.call-update) | async-done | bytes 65552 | tf_op jit(solution)/shard_map/reduce_scatter | solution.py:90
  353.8 38.7 %reduce-scatter.17.cloned.1.call-done = bf16[32,1024]{1,0:T(8,128)(2,1)} async-done(((bf16[256,1024]{1,0:T(8,128)(2,1)}), bf16[32,1024]{1,0:T(8,128)(2,1)}) %reduce-scatter.17.cloned.1.call-update) | async-done | bytes 65552 | tf_op jit(solution)/shard_map/reduce_scatter | solution.py:90
  392.5 38.7 %reduce-scatter.13.cloned.1.call-done = bf16[32,1024]{1,0:T(8,128)(2,1)} async-done(((bf16[256,1024]{1,0:T(8,128)(2,1)}), bf16[32,1024]{1,0:T(8,128)(2,1)}) %reduce-scatter.13.cloned.1.call-update) | async-done | bytes 65552 | tf_op jit(solution)/shard_map/reduce_scatter | solution.py:90
  (75 shorter events, 41.8 us)
Async XLA Ops:
  6.5 137.3 %copy-start = (bf16[1024,2,464]{0,2,1:T(8,128)(2,1)S(1)}, bf16[1024,2,464]{0,2,1:T(8,128)(2,1)}, u32[]{:S(2)}) copy-start(bf16[1024,2,464]{0,2,1:T(8,128)(2,1)} %param.8) | copy-start | bytes 5701636
  31.5 7.5 %copy-start.4 = (bf16[1,1,64,8192]{3,2,1,0:T(8,128)(2,1)S(1)}, bf16[1,1,64,8192]{3,2,1,0:T(8,128)(2,1)}, u32[]{:S(2)}) copy-start(bf16[1,1,64,8192]{3,2,1,0:T(8,128)(2,1)} %param.10) | copy-start | bytes 3145732
  32.7 21.0 %all-to-all-start = ((bf16[8,64,1024]{2,1,0:T(8,128)(2,1)}), bf16[8,64,1024]{2,1,0:T(8,128)(2,1)}, u32[]{:S(2)}, u32[]{:S(2)}) async-start(bf16[8,64,1024]{2,1,0:T(8,128)(2,1)} %bitcast.7), calls=%async_computation | async-start | bytes 2097152 | tf_op jit(solution)/shard_map/all_to_all | solution.py:46
  57.8 22.0 %all-to-all-start.1 = ((bf16[32,2,2048]{2,1,0:T(2,128)(2,1)}), bf16[32,2,2048]{2,1,0:T(2,128)(2,1)S(1)}, u32[]{:S(2)}, u32[]{:S(2)}) async-start(bf16[32,2,2048]{2,1,0:T(2,128)(2,1)} %reshape.135), calls=%async_computation.1 | async-start | bytes 524288 | tf_op jit(solution)/shard_map/all_to_all | solution.py:50
  79.8 58.0 %all-to-all-start.2 = ((bf16[32,64,464]{2,1,0:T(8,128)(2,1)}), bf16[32,64,464]{2,1,0:T(8,128)(2,1)}, u32[]{:S(2)}, u32[]{:S(2)}) async-start(bf16[32,64,464]{2,1,0:T(8,128)(2,1)} %bitcast.100), calls=%async_computation.2 | async-start | bytes 4194304 | tf_op jit(solution)/shard_map/all_to_all | solution.py:25
  140.1 1.3 copy-start.2
  141.4 2.4 copy-start.3
  146.0 1.8 copy-start.1
  148.0 2.7 collective-permute-start
  171.0 17.8 %all-to-all-start.4 = ((bf16[8,128,464]{1,2,0:T(8,128)(2,1)}), bf16[8,128,464]{1,2,0:T(8,128)(2,1)S(1)}, u32[]{:S(2)}, u32[]{:S(2)}) async-start(bf16[8,128,464]{1,2,0:T(8,128)(2,1)} %stack.13), calls=%async_computation.4 | async-start | bytes 1900544 | tf_op jit(solution)/shard_map/all_to_all | solution.py:85
  175.9 109.1 %reduce-scatter.7.cloned.1.call-start = ((), (), s32[]{:S(2)}) async-start(), calls=%async_computation.15 | async-start | bytes 2621440 | tf_op jit(solution)/shard_map/reduce_scatter | solution.py:89
  197.2 2.6 collective-permute-start.2
  218.4 17.8 %all-to-all-start.8 = ((bf16[8,128,464]{1,2,0:T(8,128)(2,1)}), bf16[8,128,464]{1,2,0:T(8,128)(2,1)S(1)}, u32[]{:S(2)}, u32[]{:S(2)}) async-start(bf16[8,128,464]{1,2,0:T(8,128)(2,1)} %stack.17), calls=%async_computation.12 | async-start | bytes 1900544 | tf_op jit(solution)/shard_map/all_to_all | solution.py:85
  223.3 62.3 %reduce-scatter.15.cloned.1.call-start = ((), (), s32[]{:S(2)}) async-start(), calls=%async_computation.19 | async-start | bytes 2621440 | tf_op jit(solution)/shard_map/reduce_scatter | solution.py:89
  240.0 73.9 %reduce-scatter.11.cloned.1.call-start = ((), (), s32[]{:S(2)}) async-start(), calls=%async_computation.17 | async-start | bytes 2621440 | tf_op jit(solution)/shard_map/reduce_scatter | solution.py:89
  244.8 2.6 collective-permute-start.1
  264.9 17.4 %copy-start.5 = (bf16[464,1024]{1,0:T(8,128)(2,1)S(1)}, bf16[464,1024]{1,0:T(8,128)(2,1)}, u32[]{:S(2)}) copy-start(bf16[464,1024]{1,0:T(8,128)(2,1)} %param.9) | copy-start | bytes 2850820
  284.9 68.9 %reduce-scatter.9.cloned.1.call-start = ((), (), s32[]{:S(2)}) async-start(), calls=%async_computation.16 | async-start | bytes 589824 | tf_op jit(solution)/shard_map/reduce_scatter | solution.py:90
  285.5 107.0 %reduce-scatter.17.cloned.1.call-start = ((), (), s32[]{:S(2)}) async-start(), calls=%async_computation.20 | async-start | bytes 589824 | tf_op jit(solution)/shard_map/reduce_scatter | solution.py:90
  286.1 145.1 %reduce-scatter.13.cloned.1.call-start = ((), (), s32[]{:S(2)}) async-start(), calls=%async_computation.18 | async-start | bytes 589824 | tf_op jit(solution)/shard_map/reduce_scatter | solution.py:90
Sparse Core Ops, SparseCore 0:
  192.8 29.2 reduce-scatter.6
  240.1 29.1 reduce-scatter.14
  285.1 28.8 reduce-scatter.10
  316.3 37.4 reduce-scatter.8
  356.2 36.2 reduce-scatter.16
  394.9 36.2 reduce-scatter.12
